TPU v7x, 32 devices: a whole 2x2x4 slice. The times are simulated.
32 devices in a mesh: rel: 4 (over y, x), node: 4 (over z), feat: 2 (over core).
Axes of the slice: x: 2, y: 2, z: 4, core: 2. Of those that a mesh axis runs over, the one named last changes fastest.
Arguments:
- features: float32 [3072, 768], P('node', 'feat'), may hold values from -6 to 6
- tile_values: float32 [4, 12, 12, 256, 256], P('rel', 'node'), may hold values from -0.4375 to 0.4375
- tile_cols: int32 [4, 12, 12], P('rel', 'node'), may hold values from 0 to 11, as said below
- tile_count: int32 [4, 12], P('rel', 'node'), may hold values from 1 to 12, as said below
- degree: int32 [4, 3072], P('rel', 'node'), may hold values from 1 to 16
- proj_weight: float32 [4, 768, 512], P('rel', 'feat'), may hold values from -0.21875 to 0.21875
- proj_bias: float32 [4, 512], P('rel', 'feat'), may hold values from -3 to 3
Outputs:
- metapath_out: float32 [4, 3072, 512], P(None, ('node', 'rel'), 'feat')
Inputs may be any that keep to these rules, and one draw needn't show every extreme that they name: `tile_cols`: within one row of tiles the 12 column tiles are distinct; slots at or past the count hold valid tile numbers that are not used. `tile_count`: in every relation some row of tiles has exactly 12 live slots.
All inputs are finite; a program needn't handle non-finite values.
Results may differ from a plain program's by a relative error of at most 0.0001.
Values sent between devices are 32-bit elements; how exact they have to be, the bound alone decides.
A program may use at most 128 MiB of HBM per device.

v0:
```python
import jax
import jax.numpy as jnp
from jax import lax
from jax.sharding import PartitionSpec as P


def spread(gathered, masked, col_tiles, row_scale):
    columns = gathered.shape[1]
    tile_rows = gathered.reshape(-1, masked.shape[2], columns)
    sources = jnp.take(tile_rows, col_tiles, axis=0)
    summed = jnp.einsum(
        "tkab,tkbw->taw",
        masked,
        sources,
        precision=lax.Precision.HIGHEST,
        preferred_element_type=jnp.float32,
    )
    return row_scale * summed.reshape(-1, columns)


def on_device(features, tile_values, tile_cols, tile_count, degree, proj_weight, proj_bias):
    row_scale = lax.rsqrt(degree[0].astype(jnp.float32))[:, None]
    counts = tile_count[0]
    live_mask = (jnp.arange(tile_values.shape[2])[None, :] < counts[:, None]).astype(jnp.float32)
    masked = tile_values[0] * live_mask[:, :, None, None]
    col_tiles = tile_cols[0]
    weight = proj_weight[0]
    current = features
    for hop_index in range(2):
        current = spread(
            lax.all_gather(row_scale * current, "node", axis=0, tiled=True),
            masked,
            col_tiles,
            row_scale,
        )
    partial_sum = jnp.dot(
        current, weight, precision=lax.Precision.HIGHEST, preferred_element_type=jnp.float32
    )
    result = lax.psum_scatter(partial_sum, "feat", scatter_dimension=1, tiled=True)
    result = result + proj_bias[0][None, :]
    regrouped = lax.all_to_all(result[None], "rel", split_axis=1, concat_axis=0, tiled=True)
    return regrouped


def solution(mesh):
    return jax.shard_map(
        on_device,
        mesh=mesh,
        in_specs=(
            P("node", "feat"),
            P("rel", "node", None, None, None),
            P("rel", "node", None),
            P("rel", "node"),
            P("rel", "node"),
            P("rel", "feat", None),
            P("rel", "feat"),
        ),
        out_specs=P(None, ("node", "rel"), "feat"),
        check_vma=False,
    )
```

profile of v0, /device:TPU:0, one launch (start us, length us, event | category | flops | bytes accessed | tf_op | source)
XLA Modules:
  0.0 290.3 jit_solution(789540401075183699)
XLA Ops:
  6.5 0.0 copy-start
  6.5 0.0 all-gather.3.cloned.1.call-start
  6.5 0.8 rsqrt_reduce_fusion
  7.3 2.5 broadcast_multiply_fusion
  9.8 0.0 all-gather.3.cloned.1.call-update
  9.8 0.0 all-gather.5.cloned.1.call-start
  9.9 0.7 compare_select_fusion
  10.5 0.1 reshape.83
  10.6 0.8 fusion.19
  11.4 90.7 %all-gather.3.cloned.1.call-done = f32[3072,384]{1,0:T(8,128)} async-done(((f32[768,384]{1,0:T(8,128)}), f32[3072,384]{1,0:T(8,128)}) %all-gather.3.cloned.1.call-update) | async-done | bytes 4718608 | tf_op jit(solution)/shard_map/all_gather | solution.py:31
  102.1 11.3 %gather_fusion = f32[36,256,384]{2,1,0:T(8,128)} fusion(f32[12,256,384]{2,1,0:T(8,128)} %bitcast.40, s32[1024]{0:T(1024)S(1)} %pad_clamp_fusion), kind=kCustom, calls=%fused_computation.clone | custom fusion | bytes 28311696 | tf_op jit(solution)/shard_map/jit(_take)/gather | solution.py:10
  113.3 20.0 %fusion.2 = f32[3,256,384,1]{2,1,3,0:T(8,128)S(1)} fusion(f32[3,12,256,384]{3,2,1,0:T(8,128)} %bitcast.39, f32[1,3,12,256,256]{4,3,2,1,0:T(8,128)} %param.10, pred[3,12]{1,0:T(4,128)(4,1)S(1)} %get-tuple-element.7, f32[3,12]{1,0:T(4,128)S(1)} %get-tuple-element.6), kind=kOutput, calls=%fused_computation.4 | convolution fusion | flops 10877534208 | bytes 24772788 | tf_op jit(solution)/shard_map/tkab,tkbw->taw/dot_general | solution.py:11
  133.3 1.2 fusion.16
  134.5 0.0 all-gather.5.cloned.1.call-update
  134.5 0.2 reduce-scatter.2.cloned.1.call-start
  134.8 87.8 %all-gather.5.cloned.1.call-done = f32[3072,384]{1,0:T(8,128)} async-done(((f32[768,384]{1,0:T(8,128)}), f32[3072,384]{1,0:T(8,128)}) %all-gather.5.cloned.1.call-update) | async-done | bytes 4718608 | tf_op jit(solution)/shard_map/all_gather | solution.py:31
  222.6 11.3 %gather_fusion.1 = f32[36,256,384]{2,1,0:T(8,128)} fusion(f32[12,256,384]{2,1,0:T(8,128)} %bitcast.41, s32[1024]{0:T(1024)S(1)} %pad_clamp_fusion), kind=kCustom, calls=%fused_computation.1.clone | custom fusion | bytes 28311696 | tf_op jit(solution)/shard_map/jit(_take)/gather | solution.py:10
  233.8 0.0 copy-start.1
  233.8 20.0 %fusion.13 = f32[3,256,384]{2,1,0:T(8,128)S(1)} fusion(f32[3,12,256,384]{3,2,1,0:T(8,128)} %bitcast.38, pred[3,12]{1,0:T(4,128)(4,1)S(1)} %get-tuple-element.7, f32[1,3,12,256,256]{4,3,2,1,0:T(8,128)} %param.10, f32[3,12]{1,0:T(4,128)S(1)} %get-tuple-element.6, f32[3,256]{1,0:T(4,128)S(1)} %rsqrt.15), kind=kOutput, calls=%fused_computation.14 | convolution fusion | flops 10877829120 | bytes 24775860 | tf_op jit(solution)/shard_map/tkab,tkbw->taw/dot_general | solution.py:11
  253.8 0.0 copy-done
  253.8 3.8 %fusion.17 = f32[768,512]{1,0:T(8,128)} fusion(f32[768,384]{1,0:T(8,128)S(1)} %bitcast.42, f32[1,384,512]{2,1,0:T(8,128)S(1)} %copy-done), kind=kOutput, calls=%fused_computation.17 | convolution fusion | flops 1811939328 | bytes 3538944 | tf_op jit(solution)/shard_map/dot_general | solution.py:36
  257.6 0.0 reduce-scatter.2.cloned.1.call-update
  257.6 7.7 %reduce-scatter.2.cloned.1.call-done = f32[768,256]{1,0:T(8,128)} async-done(((f32[768,512]{1,0:T(8,128)}), f32[768,256]{1,0:T(8,128)}) %reduce-scatter.2.cloned.1.call-update) | async-done | bytes 786448 | tf_op jit(solution)/shard_map/reduce_scatter | solution.py:39
  265.3 0.0 copy-done.1
  265.3 1.2 add_bitcast_fusion
  266.5 0.8 copy.8
  267.3 15.5 %all_to_all.12 = f32[1,768,256]{2,0,1:T(1,128)S(1)} all-to-all(f32[1,768,256]{2,0,1:T(1,128)S(1)} %copy.8), channel_id=1, replica_groups=mesh['rel'=4,'node'=4,'feat'=2] {'rel'}, dimensions={1} | all-to-all | bytes 1572864 | tf_op jit(solution)/shard_map/all_to_all | solution.py:41
  282.8 0.9 copy.12
  (2 shorter events, 0.0 us)
Async XLA Ops:
  6.5 247.3 %copy-start = (f32[1,384,512]{2,1,0:T(8,128)S(1)}, f32[1,384,512]{2,1,0:T(8,128)}, u32[]{:S(2)}) copy-start(f32[1,384,512]{2,1,0:T(8,128)} %param.14) | copy-start | bytes 2359300
  6.5 95.5 %all-gather.3.cloned.1.call-start = ((), (), s32[]{:S(2)}) async-start(), calls=%async_computation.2 | async-start | bytes 5898240 | tf_op jit(solution)/shard_map/all_gather | solution.py:31
  9.8 212.8 %all-gather.5.cloned.1.call-start = ((), (), s32[]{:S(2)}) async-start(), calls=%async_computation.3 | async-start | bytes 5898240 | tf_op jit(solution)/shard_map/all_gather | solution.py:31
  134.5 130.8 %reduce-scatter.2.cloned.1.call-start = ((), (), s32[]{:S(2)}) async-start(), calls=%async_computation.4 | async-start | bytes 2359296 | tf_op jit(solution)/shard_map/reduce_scatter | solution.py:39
  233.8 31.5 %copy-start.1 = (f32[1,256]{1,0:T(1,128)S(1)}, f32[1,256]{1,0:T(1,128)}, u32[]{:S(2)}) copy-start(f32[1,256]{1,0:T(1,128)} %param.15) | copy-start | bytes 3076
Sparse Core Ops, SparseCore 0:
  9.9 92.0 all-gather.2
  134.6 87.8 all-gather.4
  257.7 7.5 reduce-scatter.1
where the time goes:
time: 291 us; the launch traced here: 290 us
  waiting for transfers between devices  186 us (64%)
  matrix products  43.7 us (15%)
  local copies, waits for them, and re-layouts  24.4 us (8%)
  blocking collectives  15.5 us (5%)
  between operations  13.2 us (5%)
  other arithmetic  7.08 us (2%)
    all_gather x2, waiting for transfers between devices, on_device(): lax.all_gather(row_scale * current, 'node', axis=0, tiled=True)  178 us
    dot_general x2, matrix products, spread(): jnp.einsum('tkab,tkbw->taw', masked, sources, precision=lax.Precision.HIG...  39.9 us
    gather x2, local copies, waits for them, and re-layouts, spread(): sources = jnp.take(tile_rows, col_tiles, axis=0)  22.5 us
    all_to_all x1, blocking collectives, on_device(): lax.all_to_all(result[None], 'rel', split_axis=1, concat_axis=0, tiled=True)  15.5 us
    reduce_scatter x1, waiting for transfers between devices, on_device(): lax.psum_scatter(partial_sum, 'feat', scatter_dimension=1, tiled=True)  7.7 us
  transfers between devices with their start and end apart: 3, of which 3 were waited for; matrix products, arithmetic and copies ran while one was open for 1% of the time, Pallas kernels for 0%

commit v1 on v0

v1 whole, which is shorter than its diff:
```python
import jax
import jax.numpy as jnp
from jax import lax
from jax.sharding import PartitionSpec as P


def spread(gathered, masked, col_tiles):
    columns = gathered.shape[1]
    tile_rows = gathered.reshape(-1, masked.shape[2], columns)
    sources = jnp.take(tile_rows, col_tiles, axis=0)
    summed = jnp.einsum(
        "tkab,tkbw->taw",
        masked,
        sources,
        precision=lax.Precision.HIGH,
        preferred_element_type=jnp.float32,
    )
    return summed.reshape(-1, columns)


def on_device(features, tile_values, tile_cols, tile_count, degree, proj_weight, proj_bias):
    row_scale = lax.rsqrt(degree[0].astype(jnp.float32))[:, None]
    counts = tile_count[0]
    live_mask = (jnp.arange(tile_values.shape[2])[None, :] < counts[:, None]).astype(jnp.float32)
    masked = tile_values[0] * live_mask[:, :, None, None]
    col_tiles = tile_cols[0]
    partial_sum = jnp.dot(
        features, proj_weight[0], precision=lax.Precision.HIGH, preferred_element_type=jnp.float32
    )
    current = lax.psum_scatter(partial_sum, "feat", scatter_dimension=1, tiled=True)
    for hop_index in range(2):
        gathered = lax.all_gather(row_scale * current, "node", axis=0, tiled=True)
        current = row_scale * spread(gathered, masked, col_tiles)
    result = current + proj_bias[0][None, :]
    return lax.all_to_all(result[None], "rel", split_axis=1, concat_axis=0, tiled=True)


def solution(mesh):
    return jax.shard_map(
        on_device,
        mesh=mesh,
        in_specs=(
            P("node", "feat"),
            P("rel", "node", None, None, None),
            P("rel", "node", None),
            P("rel", "node"),
            P("rel", "node"),
            P("rel", "feat", None),
            P("rel", "feat"),
        ),
        out_specs=P(None, ("node", "rel"), "feat"),
        check_vma=False,
    )
```

time: 291 us -> 217 us (0.75)
  waiting for transfers between devices: 186 us -> 137 us
  matrix products: 43.7 us -> 25.6 us
  local copies, waits for them, and re-layouts: 24.4 us -> 20.3 us
    all_gather x2, waiting for transfers between devices: 178 us -> 126 us  [on_device(): gathered = lax.all_gather(row_scale * current, 'node', axis=0, tiled=True)]
    dot_general x2, matrix products: 39.9 us -> 21.9 us  [spread(): jnp.einsum('tkab,tkbw->taw', masked, sources, precision=lax.Precision.HIG...]
    gather x2, local copies, waits for them, and re-layouts: 22.5 us -> 17.2 us  [spread(): sources = jnp.take(tile_rows, col_tiles, axis=0)]
    reduce_scatter x1, waiting for transfers between devices: 7.7 us -> 11.1 us  [on_device(): lax.psum_scatter(partial_sum, 'feat', scatter_dimension=1, tiled=True)]
where the time goes in v1:
time: 217 us; the launch traced here: 216 us
  waiting for transfers between devices  137 us (63%)
  matrix products  25.6 us (12%)
  local copies, waits for them, and re-layouts  20.3 us (9%)
  blocking collectives  14.7 us (7%)
  between operations  13.2 us (6%)
  other arithmetic  5.56 us (3%)
    all_gather x2, waiting for transfers between devices, on_device(): gathered = lax.all_gather(row_scale * current, 'node', axis=0, tiled=True)  126 us
    dot_general x2, matrix products, spread(): jnp.einsum('tkab,tkbw->taw', masked, sources, precision=lax.Precision.HIG...  21.9 us
    gather x2, local copies, waits for them, and re-layouts, spread(): sources = jnp.take(tile_rows, col_tiles, axis=0)  17.2 us
    all_to_all x1, blocking collectives, on_device(): lax.all_to_all(result[None], 'rel', split_axis=1, concat_axis=0, tiled=True)  14.7 us
    reduce_scatter x1, waiting for transfers between devices, on_device(): lax.psum_scatter(partial_sum, 'feat', scatter_dimension=1, tiled=True)  11.1 us
  transfers between devices with their start and end apart: 3, of which 3 were waited for; matrix products, arithmetic and copies ran while one was open for 1% of the time, Pallas kernels for 0%

profile of v1, /device:TPU:0, one launch (start us, length us, event | category | flops | bytes accessed | tf_op | source)
XLA Modules:
  0.0 216.2 jit_solution(5188851948771330307)
XLA Ops:
  6.5 0.0 copy-start
  6.5 0.0 reduce-scatter.2.cloned.1.call-start
  6.5 1.3 copy-done
  7.8 3.7 %fusion.11 = f32[768,512]{1,0:T(8,128)} fusion(f32[768,384]{1,0:T(8,128)S(1)} %copy-done, f32[1,384,512]{2,1,0:T(8,128)} %param.14), kind=kOutput, calls=%fused_computation.15 | convolution fusion | flops 905969664 | bytes 3538944 | tf_op jit(solution)/shard_map/dot_general | solution.py:27
  11.5 0.0 reduce-scatter.2.cloned.1.call-update
  11.5 0.0 all-gather.3.cloned.1.call-start
  11.6 0.7 rsqrt_reduce_fusion
  12.3 11.1 %reduce-scatter.2.cloned.1.call-done = f32[768,256]{1,0:T(8,128)} async-done(((f32[768,512]{1,0:T(8,128)}), f32[768,256]{1,0:T(8,128)}) %reduce-scatter.2.cloned.1.call-update) | async-done | bytes 786448 | tf_op jit(solution)/shard_map/reduce_scatter | solution.py:30
  23.4 2.2 %broadcast_multiply_fusion = f32[768,256]{1,0:T(8,128)} fusion(f32[768,256]{1,0:T(8,128)} %reduce-scatter.2.cloned.1.call-done, f32[768]{0:T(1024)S(1)} %rsqrt_reduce_fusion), kind=kLoop, calls=%fused_computation.18 | loop fusion | flops 196608 | bytes 1575936 | tf_op jit(solution)/shard_map/mul | solution.py:32
  25.6 0.0 all-gather.3.cloned.1.call-update
  25.6 0.0 all-gather.5.cloned.1.call-start
  25.7 0.7 compare_select_fusion
  26.4 0.1 reshape.133
  26.5 0.8 fusion.13
  27.2 63.3 %all-gather.3.cloned.1.call-done = f32[3072,256]{1,0:T(8,128)} async-done(((f32[768,256]{1,0:T(8,128)}), f32[3072,256]{1,0:T(8,128)}) %all-gather.3.cloned.1.call-update) | async-done | bytes 3145744 | tf_op jit(solution)/shard_map/all_gather | solution.py:32
  90.5 8.6 %gather_fusion = f32[36,256,256]{2,1,0:T(8,128)} fusion(f32[12,256,256]{2,1,0:T(8,128)} %bitcast.32, s32[1024]{0:T(1024)S(1)} %pad_clamp_fusion), kind=kCustom, calls=%fused_computation.clone | custom fusion | bytes 18874512 | tf_op jit(solution)/shard_map/jit(_take)/gather | solution.py:10
  99.1 11.0 %fusion.2 = f32[3,256,256,1]{2,1,3,0:T(8,128)S(1)} fusion(f32[3,12,256,256]{3,2,1,0:T(8,128)} %bitcast.31, f32[1,3,12,256,256]{4,3,2,1,0:T(8,128)} %param.10, f32[3,12]{1,0:T(4,128)S(1)} %get-tuple-element.6, pred[3,12]{1,0:T(4,128)(4,1)S(1)} %get-tuple-element.7), kind=kOutput, calls=%fused_computation.5 | convolution fusion | flops 3628597248 | bytes 19660980 | tf_op jit(solution)/shard_map/tkab,tkbw->taw/dot_general | solution.py:11
  110.1 1.1 fusion.10
  111.1 0.0 all-gather.5.cloned.1.call-update
  111.2 62.3 %all-gather.5.cloned.1.call-done = f32[3072,256]{1,0:T(8,128)} async-done(((f32[768,256]{1,0:T(8,128)}), f32[3072,256]{1,0:T(8,128)}) %all-gather.5.cloned.1.call-update) | async-done | bytes 3145744 | tf_op jit(solution)/shard_map/all_gather | solution.py:32
  173.5 8.6 %gather_fusion.1 = f32[36,256,256]{2,1,0:T(8,128)} fusion(f32[12,256,256]{2,1,0:T(8,128)} %bitcast.33, s32[1024]{0:T(1024)S(1)} %pad_clamp_fusion), kind=kCustom, calls=%fused_computation.1.clone | custom fusion | bytes 18874512 | tf_op jit(solution)/shard_map/jit(_take)/gather | solution.py:10
  182.1 0.0 copy-start.1
  182.1 11.0 %fusion = f32[3,256,256,1]{2,1,3,0:T(8,128)S(1)} fusion(f32[3,12,256,256]{3,2,1,0:T(8,128)} %bitcast.30, f32[1,3,12,256,256]{4,3,2,1,0:T(8,128)} %param.10, f32[3,12]{1,0:T(4,128)S(1)} %get-tuple-element.6, pred[3,12]{1,0:T(4,128)(4,1)S(1)} %get-tuple-element.7), kind=kOutput, calls=%fused_computation.3 | convolution fusion | flops 3628597248 | bytes 19660980 | tf_op jit(solution)/shard_map/tkab,tkbw->taw/dot_general | solution.py:11
  193.1 0.0 copy-done.1
  193.1 0.2 multiply_add_fusion
  193.2 0.8 copy.9
  194.1 14.7 %all_to_all.12 = f32[1,768,256]{2,0,1:T(1,128)S(1)} all-to-all(f32[1,768,256]{2,0,1:T(1,128)S(1)} %copy.9), channel_id=1, replica_groups=mesh['rel'=4,'node'=4,'feat'=2] {'rel'}, dimensions={1} | all-to-all | bytes 1572864 | tf_op jit(solution)/shard_map/all_to_all | solution.py:35
  208.8 0.9 copy.13
  (1 shorter events, 0.0 us)
Async XLA Ops:
  6.5 1.3 copy-start
  6.5 16.9 %reduce-scatter.2.cloned.1.call-start = ((), (), s32[]{:S(2)}) async-start(), calls=%async_computation.2 | async-start | bytes 2359296 | tf_op jit(solution)/shard_map/reduce_scatter | solution.py:30
  11.5 79.0 %all-gather.3.cloned.1.call-start = ((), (), s32[]{:S(2)}) async-start(), calls=%async_computation.3 | async-start | bytes 3932160 | tf_op jit(solution)/shard_map/all_gather | solution.py:32
  25.6 147.8 %all-gather.5.cloned.1.call-start = ((), (), s32[]{:S(2)}) async-start(), calls=%async_computation.4 | async-start | bytes 3932160 | tf_op jit(solution)/shard_map/all_gather | solution.py:32
  182.1 11.0 %copy-start.1 = (f32[1,256]{1,0:T(1,128)S(1)}, f32[1,256]{1,0:T(1,128)}, u32[]{:S(2)}) copy-start(f32[1,256]{1,0:T(1,128)} %param.15) | copy-start | bytes 3076
Sparse Core Ops, SparseCore 0:
  11.6 11.7 reduce-scatter.1
  25.8 64.7 all-gather.2
  111.3 62.1 all-gather.4

commit v2 on v1

v2 whole, which is shorter than its diff:
```python
import functools

import jax
import jax.numpy as jnp
from jax import lax
from jax.experimental import pallas as pl
from jax.experimental.pallas import tpu as pltpu
from jax.sharding import PartitionSpec as P

MESH = pl.DeviceIdType.MESH
LANES = 128
HOPS = 2


def split(x):
    high = x.astype(jnp.bfloat16)
    return high, (x - high.astype(jnp.float32)).astype(jnp.bfloat16)


def paired(x):
    high, low = split(x)
    return high, jnp.concatenate([high, low], axis=1)


def product(a, x_high, x_pair):
    a_high, a_low = split(a)
    both = jnp.dot(a_high, x_pair, preferred_element_type=jnp.float32)
    rest = jnp.dot(a_low, x_high, preferred_element_type=jnp.float32)
    return both[:, :LANES] + both[:, LANES:] + rest


def kernel(
    sizes,
    slot_of,
    live,
    features,
    weight,
    scale,
    bias,
    tiles_hbm,
    out,
    tiles,
    field,
    total,
    result,
    partial_out,
    partial_in,
    tiles_sem,
    pair_send,
    pair_recv,
    line_send,
    line_recv,
    out_send,
    out_recv,
):
    nodes, rels, chunks = sizes
    rows = features.shape[0]
    tile = tiles.shape[2]
    row_tiles = tiles.shape[0]
    col_tiles = nodes * row_tiles
    group = rows // rels
    rel, node, feat = (lax.axis_index(name) for name in ("rel", "node", "feat"))
    has_up, has_down = node < nodes - 1, node > 0

    tiles_copy = pltpu.make_async_copy(tiles_hbm, tiles, tiles_sem)
    tiles_copy.start()

    barrier = pltpu.get_barrier_semaphore()
    pl.semaphore_signal(barrier, inc=1, device_id={"feat": 1 - feat}, device_id_type=MESH)
    for step in range(1, rels):
        peer = lax.rem(rel + step, rels)
        pl.semaphore_signal(barrier, inc=1, device_id={"rel": peer}, device_id_type=MESH)

    @pl.when(has_up)
    def _():
        pl.semaphore_signal(barrier, inc=1, device_id={"node": node + 1}, device_id_type=MESH)

    @pl.when(has_down)
    def _():
        pl.semaphore_signal(barrier, inc=1, device_id={"node": node - 1}, device_id_type=MESH)

    peers = rels + has_up.astype(jnp.int32) + has_down.astype(jnp.int32)
    pl.semaphore_wait(barrier, peers)

    def line_copy(stage, way, slot):
        neighbour = node + 1 if way == 0 else node - 1
        return pltpu.make_async_remote_copy(
            src_ref=field.at[stage, slot],
            dst_ref=field.at[stage, slot],
            send_sem=line_send.at[stage, way, slot],
            recv_sem=line_recv.at[stage, slot],
            device_id={"node": neighbour},
            device_id_type=MESH,
        )

    def send_up(stage, slot):
        @pl.when(has_up)
        def _():
            line_copy(stage, 0, slot).start()

    def send_down(stage, slot):
        @pl.when(has_down)
        def _():
            line_copy(stage, 1, slot).start()

    def accumulate(stage, slot):
        def one_tile(j, carry):
            x = field[stage, slot, pl.ds(pl.multiple_of(j * tile, tile), tile), :]
            x_high, x_pair = paired(x)
            for t in range(row_tiles):
                place = t * col_tiles + slot * row_tiles + j
                a = tiles[t, slot_of[place]] * live[place]
                total[t * tile : (t + 1) * tile, :] += product(a, x_high, x_pair)
            return carry

        lax.fori_loop(0, row_tiles, one_tile, 0)

    def hop(stage):
        total[...] = jnp.zeros_like(total)
        accumulate(stage, node)

        def step(s, carry):
            @pl.when(node - s >= 0)
            def _():
                line_copy(stage, 0, node - s).wait_recv()
                send_up(stage, node - s)

            @pl.when(node + s < nodes)
            def _():
                line_copy(stage, 1, node + s).wait_recv()
                send_down(stage, node + s)

            @pl.when(node - s >= 0)
            def _():
                accumulate(stage, node - s)

            @pl.when(node + s < nodes)
            def _():
                accumulate(stage, node + s)

            return carry

        lax.fori_loop(1, nodes, step, 0)

    def begin(stage):
        send_up(stage, node)
        send_down(stage, node)

    def project(side, chunk, target):
        start = pl.multiple_of((side * chunks + chunk) * LANES, LANES)
        w_high, w_pair = paired(weight[:, pl.ds(start, LANES)])

        def some_rows(j, carry):
            place = pl.ds(pl.multiple_of(j * tile, tile), tile)
            target(place, product(features[place, :], w_high, w_pair))
            return carry

        lax.fori_loop(0, row_tiles, some_rows, 0)

    def pair_copy(chunk):
        return pltpu.make_async_remote_copy(
            src_ref=partial_out.at[chunk],
            dst_ref=partial_in.at[chunk],
            send_sem=pair_send.at[chunk],
            recv_sem=pair_recv.at[chunk],
            device_id={"feat": 1 - feat},
            device_id_type=MESH,
        )

    for chunk in range(chunks):

        def keep_out(place, value, chunk=chunk):
            partial_out[chunk, place, :] = value

        project(1 - feat, chunk, keep_out)
        pair_copy(chunk).start()
    for chunk in range(chunks):

        def keep_own(place, value, chunk=chunk):
            field[chunk, node, place, :] = value

        project(feat, chunk, keep_own)
        pair_copy(chunk).wait_recv()
        field[chunk, node] = scale[...] * (field[chunk, node] + partial_in[chunk])
        begin(chunk)

    tiles_copy.wait()

    for chunk in range(chunks):
        hop(chunk)
        field[chunks + chunk, node] = scale[...] * (scale[...] * total[...])
        begin(chunks + chunk)

    def out_copy(chunk, step):
        peer = lax.rem(rel + step, rels)
        return pltpu.make_async_remote_copy(
            src_ref=result.at[chunk, pl.ds(pl.multiple_of(peer * group, 8), group), :],
            dst_ref=out.at[rel, :, pl.ds(chunk * LANES, LANES)],
            send_sem=out_send.at[chunk, step],
            recv_sem=out_recv.at[chunk, step],
            device_id={"rel": peer},
            device_id_type=MESH,
        )

    def in_copy(chunk, step):
        peer = lax.rem(rel + rels - step, rels)
        return pltpu.make_async_remote_copy(
            src_ref=result.at[chunk, pl.ds(0, group), :],
            dst_ref=out.at[peer, :, pl.ds(chunk * LANES, LANES)],
            send_sem=out_send.at[chunk, step],
            recv_sem=out_recv.at[chunk, step],
            device_id={"rel": peer},
            device_id_type=MESH,
        )

    for chunk in range(chunks):
        hop(chunks + chunk)
        columns = slice(chunk * LANES, (chunk + 1) * LANES)
        result[chunk] = scale[...] * total[...] + bias[:, columns]
        for step in range(1, rels):
            out_copy(chunk, step).start()
        own = pl.ds(pl.multiple_of(rel * group, 8), group)
        out[rel, :, columns] = result[chunk, own, :]

    for chunk in range(chunks):
        pair_copy(chunk).wait_send()
        for step in range(1, rels):
            out_copy(chunk, step).wait_send()
            in_copy(chunk, step).wait_recv()
    for stage in range(HOPS * chunks):

        def drain(slot, carry, stage=stage):
            @pl.when(jnp.logical_and(has_up, slot <= node))
            def _():
                line_copy(stage, 0, slot).wait_send()

            @pl.when(jnp.logical_and(has_down, slot >= node))
            def _():
                line_copy(stage, 1, slot).wait_send()

            return carry

        lax.fori_loop(0, nodes, drain, 0)


def on_device(
    nodes, rels, features, tile_values, tile_cols, tile_count, degree, proj_weight, proj_bias
):
    rows, depth = features.shape
    _, row_tiles, slots, tile, _ = tile_values.shape
    width = proj_bias.shape[1]
    chunks = width // LANES
    col_tiles = nodes * row_tiles
    stages = HOPS * chunks
    scale = jnp.broadcast_to(lax.rsqrt(degree[0].astype(jnp.float32))[:, None], (rows, LANES))
    places = jnp.arange(slots)
    used = places[None, :] < tile_count[0][:, None]
    hit = (tile_cols[0][:, None, :] == jnp.arange(col_tiles)[None, :, None]) & used[:, None, :]
    slot_of = jnp.sum(jnp.where(hit, places[None, None, :], 0), axis=2).astype(jnp.int32)
    live = jnp.sum(hit.astype(jnp.float32), axis=2)
    vmem = pl.BlockSpec(memory_space=pltpu.VMEM)
    smem = pl.BlockSpec(memory_space=pltpu.SMEM)
    dma = pltpu.SemaphoreType.DMA
    return pl.pallas_call(
        functools.partial(kernel, (nodes, rels, chunks)),
        out_shape=jax.ShapeDtypeStruct((rels, rows // rels, width), jnp.float32),
        in_specs=[smem, smem, vmem, vmem, vmem, vmem, pl.BlockSpec(memory_space=pl.ANY)],
        out_specs=vmem,
        scratch_shapes=[
            pltpu.VMEM((row_tiles, slots, tile, tile), jnp.float32),
            pltpu.VMEM((stages, nodes, rows, LANES), jnp.float32),
            pltpu.VMEM((rows, LANES), jnp.float32),
            pltpu.VMEM((chunks, rows, LANES), jnp.float32),
            pltpu.VMEM((chunks, rows, LANES), jnp.float32),
            pltpu.VMEM((chunks, rows, LANES), jnp.float32),
            dma,
            dma((chunks,)),
            dma((chunks,)),
            dma((stages, 2, nodes)),
            dma((stages, nodes)),
            dma((chunks, rels)),
            dma((chunks, rels)),
        ],
        compiler_params=pltpu.CompilerParams(
            collective_id=0, has_side_effects=True, vmem_limit_bytes=56 << 20
        ),
    )(
        slot_of.reshape(-1),
        live.reshape(-1),
        features,
        proj_weight[0],
        scale,
        proj_bias,
        tile_values[0],
    )


def solution(mesh):
    return jax.shard_map(
        functools.partial(on_device, mesh.shape["node"], mesh.shape["rel"]),
        mesh=mesh,
        in_specs=(
            P("node", "feat"),
            P("rel", "node", None, None, None),
            P("rel", "node", None),
            P("rel", "node"),
            P("rel", "node"),
            P("rel", "feat", None),
            P("rel", "feat"),
        ),
        out_specs=P(None, ("node", "rel"), "feat"),
        check_vma=False,
    )
```

time: 217 us -> 128 us (0.59)
  waiting for transfers between devices: 137 us -> 0 us
  Pallas kernels: 0 us -> 121 us
  matrix products: 25.6 us -> 0 us
  local copies, waits for them, and re-layouts: 20.3 us -> 4.89 us
  blocking collectives: 14.7 us -> 0 us
  between operations: 13.2 us -> 0.02 us
  other arithmetic: 5.56 us -> 1.67 us
    all_gather x2 -> x0, waiting for transfers between devices: 126 us -> none  [on_device(): gathered = lax.all_gather(row_scale * current, 'node', axis=0, tiled=True)]
    pallas_call x0 -> x1, Pallas kernels: none -> 121 us  [on_device(): pl.pallas_call(functools.partial(kernel, (nodes, rels, chunks)), out_shap...]
    dot_general x3 -> x0, matrix products: 25.6 us -> none  [the longest x2 21.9 us: spread(): jnp.einsum('tkab,tkbw->taw', masked, sources, precision=lax.Precision.HIG...]
    gather x2 -> x0, local copies, waits for them, and re-layouts: 17.2 us -> none  [spread(): sources = jnp.take(tile_rows, col_tiles, axis=0)]
    all_to_all x1 -> x0, blocking collectives: 14.7 us -> none  [on_device(): lax.all_to_all(result[None], 'rel', split_axis=1, concat_axis=0, tiled=True)]
    reduce_scatter x1 -> x0, waiting for transfers between devices: 11.1 us -> none  [on_device(): lax.psum_scatter(partial_sum, 'feat', scatter_dimension=1, tiled=True)]
    mul x2 -> x0, other arithmetic: 3.23 us -> none  [on_device(): gathered = lax.all_gather(row_scale * current, 'node', axis=0, tiled=True)]
  transfers between devices with their start and end apart: 3 -> 0, of which waited for: 3 -> 0; matrix products, arithmetic and copies ran while one was open for 1% -> 0% of each run, Pallas kernels for 0% -> 0%
where the time goes in v2:
time: 128 us; the launch traced here: 127 us
  Pallas kernels  121 us (95%)
  local copies, waits for them, and re-layouts  4.89 us (4%)
  other arithmetic  1.67 us (1%)
    pallas_call x1, Pallas kernels, on_device(): pl.pallas_call(functools.partial(kernel, (nodes, rels, chunks)), out_shap...  121 us
    unnamed x2, local copies, waits for them, and re-layouts  2.74 us

profile of v2, /device:TPU:0, one launch (start us, length us, event | category | flops | bytes accessed | tf_op | source)
XLA Modules:
  0.0 127.4 jit_solution(18401079692874986651)
XLA Ops:
  0.0 0.7 iota_compare_fusion.1
  0.7 0.7 copy.10
  1.4 0.1 convert_reduce_fusion
  1.5 0.6 reshape.36.live
  2.1 0.1 select_reduce_fusion
  2.2 0.7 reshape.35.slot_of
  2.9 0.7 rsqrt_reduce_fusion
  3.6 0.9 broadcast_in_dim.24.scale
  4.5 120.8 %shard_map.73 = f32[4,192,256]{2,1,0:T(8,128)} custom-call(s32[36]{0:T(128)} %reshape.35.slot_of, f32[36]{0:T(128)} %reshape.36.live, f32[768,384]{1,0:T(8,128)} %features.1, f32[384,512]{1,0:T(8,128)} %bitcast.7, f32[768,128]{1,0:T(8,128)} %broadcast_in_dim.24.scale, f32[1,256]{1,0:T(1,128)} %bias.1, f32[3,12,256,256]{3,2,1,0:T(8,128)} %bitcast.6), custom_call_target="tpu_custom_call" | custom-call | tf_op jit(solution)/shard_map/pallas_call | solution.py:264
  125.3 2.1 %copy.12 = f32[4,192,256]{2,1,0:T(8,128)} copy(f32[4,192,256]{2,1,0:T(8,128)} %shard_map.73) | data formatting | bytes 1572864

commit v3 on v2

v3 whole, which is shorter than its diff:
```python
import functools

import jax
import jax.numpy as jnp
from jax import lax
from jax.experimental import pallas as pl
from jax.experimental.pallas import tpu as pltpu
from jax.sharding import PartitionSpec as P

MESH = pl.DeviceIdType.MESH
LANES = 128
SUBLANES = 8


def split(x):
    high = x.astype(jnp.bfloat16)
    return high, (x - high.astype(jnp.float32)).astype(jnp.bfloat16)


def paired(x):
    high, low = split(x)
    return high, jnp.concatenate([high, low], axis=1)


def product(a, x_high, x_pair):
    a_high, a_low = split(a)
    width = x_high.shape[1]
    both = jnp.dot(a_high, x_pair, preferred_element_type=jnp.float32)
    rest = jnp.dot(a_low, x_high, preferred_element_type=jnp.float32)
    return both[:, :width] + both[:, width:] + rest


def kernel(
    sizes,
    slot_of,
    live,
    source_scale,
    weight,
    scale,
    bias,
    features_hbm,
    tiles_hbm,
    out,
    tiles,
    raw,
    scales,
    first,
    field,
    total,
    result,
    partial_out,
    partial_in,
    load_sem,
    scale_send,
    scale_recv,
    z_send,
    z_recv,
    x_send,
    x_recv,
    y_send,
    y_recv,
    pair_send,
    pair_recv,
    line_send,
    line_recv,
    out_send,
    out_recv,
):
    nodes, rels, chunks = sizes
    rows, depth = raw.shape[1:]
    tile = tiles.shape[2]
    row_tiles = tiles.shape[0]
    col_tiles = nodes * row_tiles
    group = rows // rels
    parts = depth // LANES
    rel, node, feat = (lax.axis_index(name) for name in ("rel", "node", "feat"))
    has_up, has_down = node < nodes - 1, node > 0
    x_rel, y_rel, far_rel = rel + 1 - 2 * lax.rem(rel, 2), lax.rem(rel + 2, rels), rels - 1 - rel

    barrier = pltpu.get_barrier_semaphore()
    pl.semaphore_signal(barrier, inc=1, device_id={"feat": 1 - feat}, device_id_type=MESH)
    for step in range(1, rels):
        peer = lax.rem(rel + step, rels)
        pl.semaphore_signal(barrier, inc=1, device_id={"rel": peer}, device_id_type=MESH)
    for step in range(1, nodes):
        peer = lax.rem(node + step, nodes)
        pl.semaphore_signal(barrier, inc=1, device_id={"node": peer}, device_id_type=MESH)
    features_copy = pltpu.make_async_copy(features_hbm, raw.at[node], load_sem.at[0])
    features_copy.start()
    tiles_copy = pltpu.make_async_copy(tiles_hbm, tiles, load_sem.at[1])
    tiles_copy.start()
    scales[node] = source_scale[...]
    features_copy.wait()
    pl.semaphore_wait(barrier, rels + nodes - 1)

    def remote(src, dst, send_sem, recv_sem, **device):
        return pltpu.make_async_remote_copy(
            src_ref=src,
            dst_ref=dst,
            send_sem=send_sem,
            recv_sem=recv_sem,
            device_id=device,
            device_id_type=MESH,
        )

    def scale_copy(slot, step):
        peer = lax.rem(node + step, nodes)
        return remote(
            scales.at[slot], scales.at[slot], scale_send.at[step], scale_recv.at[slot], node=peer
        )

    def piece(slot, quarter, part):
        place = pl.ds(pl.multiple_of(quarter * group, 8), group)
        return raw.at[slot, place, pl.ds(part * LANES, LANES)]

    def z_copy(way, slot, p):
        ref = piece(slot, rel, p) if p < parts else piece(slot, far_rel, 0)
        neighbour = node + 1 if way == 0 else node - 1
        return remote(ref, ref, z_send.at[way, slot, p], z_recv.at[slot, p], node=neighbour)

    def x_copy(slot, p, near, far):
        ref = piece(slot, near, p) if p < parts else piece(slot, far, 1)
        return remote(ref, ref, x_send.at[slot, p], x_recv.at[slot, p], rel=x_rel)

    def y_copy(slot, p, near, far):
        ref = piece(slot, near, p) if p < parts else piece(slot, far, 2)
        return remote(ref, ref, y_send.at[slot, p], y_recv.at[slot, p], rel=y_rel)

    def x_out(slot, p):
        return x_copy(slot, p, rel, y_rel)

    def x_in(slot, p):
        return x_copy(slot, p, x_rel, far_rel)

    def y_out(slot, p):
        return y_copy(slot, p, rel, x_rel)

    def y_in(slot, p):
        return y_copy(slot, p, y_rel, far_rel)

    def take_z(way, slot):
        onward = has_up if way == 0 else has_down
        for p in range(parts + 1):
            z_copy(way, slot, p).wait_recv()

            @pl.when(onward)
            def _(p=p):
                z_copy(way, slot, p).start()

            if p < parts:
                x_out(slot, p).start()
                y_out(slot, p).start()

    def take_xy(slot):
        for p in range(parts):
            x_in(slot, p).wait_recv()
            if p == 2:
                y_out(slot, parts).start()
            y_in(slot, p).wait_recv()
            if p == 1:
                x_out(slot, parts).start()
        x_in(slot, parts).wait_recv()
        y_in(slot, parts).wait_recv()

    def both_sides(s, act):
        @pl.when(node - s >= 0)
        def _():
            act(0, node - s)

        @pl.when(node + s < nodes)
        def _():
            act(1, node + s)

    for step in range(1, nodes):
        scale_copy(node, step).start()
    for p in range(parts + 1):

        @pl.when(has_up)
        def _(p=p):
            z_copy(0, node, p).start()

        @pl.when(has_down)
        def _(p=p):
            z_copy(1, node, p).start()

    def accumulate_first(slot):
        def one_tile(j, carry):
            x = raw[slot, pl.ds(pl.multiple_of(j * tile, tile), tile), :]
            x_high, x_pair = paired(x)
            column_scale = scales[slot, pl.ds(j, 1), :]
            for t in range(row_tiles):
                place = t * col_tiles + slot * row_tiles + j
                a = tiles[t, slot_of[place]] * (column_scale * live[place])
                first[t * tile : (t + 1) * tile, :] += product(a, x_high, x_pair)
            return carry

        lax.fori_loop(0, row_tiles, one_tile, 0)

    both_sides(1, take_z)
    first[...] = jnp.zeros_like(first)
    tiles_copy.wait()
    accumulate_first(node)

    def first_step(s, carry):
        both_sides(s + 1, take_z)
        both_sides(s, lambda way, slot: take_xy(slot))

        def use(way, slot):
            scale_copy(slot, 1).wait_recv()
            accumulate_first(slot)

        both_sides(s, use)
        return carry

    lax.fori_loop(1, nodes, first_step, 0)

    def line_copy(stage, way, slot):
        neighbour = node + 1 if way == 0 else node - 1
        ref = field.at[stage, slot]
        return remote(
            ref, ref, line_send.at[stage, way, slot], line_recv.at[stage, slot], node=neighbour
        )

    def send_up(stage, slot):
        @pl.when(has_up)
        def _():
            line_copy(stage, 0, slot).start()

    def send_down(stage, slot):
        @pl.when(has_down)
        def _():
            line_copy(stage, 1, slot).start()

    def accumulate(stage, slot):
        def one_tile(j, carry):
            x = field[stage, slot, pl.ds(pl.multiple_of(j * tile, tile), tile), :]
            x_high, x_pair = paired(x)
            for t in range(row_tiles):
                place = t * col_tiles + slot * row_tiles + j
                a = tiles[t, slot_of[place]] * live[place]
                total[t * tile : (t + 1) * tile, :] += product(a, x_high, x_pair)
            return carry

        lax.fori_loop(0, row_tiles, one_tile, 0)

    def hop(stage):
        total[...] = jnp.zeros_like(total)
        accumulate(stage, node)

        def step(s, carry):
            @pl.when(node - s >= 0)
            def _():
                line_copy(stage, 0, node - s).wait_recv()
                send_up(stage, node - s)

            @pl.when(node + s < nodes)
            def _():
                line_copy(stage, 1, node + s).wait_recv()
                send_down(stage, node + s)

            both_sides(s, lambda way, slot: accumulate(stage, slot))
            return carry

        lax.fori_loop(1, nodes, step, 0)

    def project(side, chunk, target):
        start = pl.multiple_of((side * chunks + chunk) * LANES, LANES)
        w_high, w_pair = paired(weight[:, pl.ds(start, LANES)])

        def some_rows(j, carry):
            place = pl.ds(pl.multiple_of(j * tile, tile), tile)
            target[place, :] = product(first[place, :], w_high, w_pair)
            return carry

        lax.fori_loop(0, row_tiles, some_rows, 0)

    def pair_copy(chunk):
        return remote(
            partial_out.at[chunk],
            partial_in.at[chunk],
            pair_send.at[chunk],
            pair_recv.at[chunk],
            feat=1 - feat,
        )

    def give(chunk):
        project(1 - feat, chunk, partial_out.at[chunk])
        pair_copy(chunk).start()

    give(0)
    for chunk in range(chunks):
        project(feat, chunk, field.at[chunk, node])
        if chunk + 1 < chunks:
            give(chunk + 1)
        pair_copy(chunk).wait_recv()
        field[chunk, node] = scale[...] * (
            scale[...] * (field[chunk, node] + partial_in[chunk])
        )
        send_up(chunk, node)
        send_down(chunk, node)

    def out_copy(chunk, step):
        peer = lax.rem(rel + step, rels)
        return remote(
            result.at[chunk, pl.ds(pl.multiple_of(peer * group, 8), group), :],
            out.at[rel, :, pl.ds(chunk * LANES, LANES)],
            out_send.at[chunk, step],
            out_recv.at[chunk, step],
            rel=peer,
        )

    def in_copy(chunk, step):
        peer = lax.rem(rel + rels - step, rels)
        return remote(
            result.at[chunk, pl.ds(0, group), :],
            out.at[peer, :, pl.ds(chunk * LANES, LANES)],
            out_send.at[chunk, step],
            out_recv.at[chunk, step],
            rel=peer,
        )

    for chunk in range(chunks):
        hop(chunk)
        columns = slice(chunk * LANES, (chunk + 1) * LANES)
        result[chunk] = scale[...] * total[...] + bias[:, columns]
        for step in range(1, rels):
            out_copy(chunk, step).start()
        own = pl.ds(pl.multiple_of(rel * group, 8), group)
        out[rel, :, columns] = result[chunk, own, :]

    for step in range(1, nodes):
        scale_copy(node, step).wait_send()

    def drain(slot, carry):
        def waits(way):
            for p in range(parts + 1):
                z_copy(way, slot, p).wait_send()
            for stage in range(chunks):
                line_copy(stage, way, slot).wait_send()

        @pl.when(jnp.logical_and(has_up, slot <= node))
        def _():
            waits(0)

        @pl.when(jnp.logical_and(has_down, slot >= node))
        def _():
            waits(1)

        @pl.when(slot != node)
        def _():
            for p in range(parts + 1):
                x_out(slot, p).wait_send()
                y_out(slot, p).wait_send()

        return carry

    lax.fori_loop(0, nodes, drain, 0)
    for chunk in range(chunks):
        pair_copy(chunk).wait_send()
        for step in range(1, rels):
            out_copy(chunk, step).wait_send()
            in_copy(chunk, step).wait_recv()


def on_device(
    nodes, rels, features, tile_values, tile_cols, tile_count, degree, proj_weight, proj_bias
):
    rows, depth = features.shape
    _, row_tiles, slots, tile, _ = tile_values.shape
    width = proj_bias.shape[1]
    chunks = width // LANES
    col_tiles = nodes * row_tiles
    parts = depth // LANES + 1
    row_scale = lax.rsqrt(degree[0].astype(jnp.float32))
    scale = jnp.broadcast_to(row_scale[:, None], (rows, LANES))
    source_scale = jnp.pad(row_scale.reshape(row_tiles, tile), ((0, SUBLANES - row_tiles), (0, 0)))
    places = jnp.arange(slots)
    used = places[None, :] < tile_count[0][:, None]
    hit = (tile_cols[0][:, None, :] == jnp.arange(col_tiles)[None, :, None]) & used[:, None, :]
    slot_of = jnp.sum(jnp.where(hit, places[None, None, :], 0), axis=2).astype(jnp.int32)
    live = jnp.sum(hit.astype(jnp.float32), axis=2)
    vmem = pl.BlockSpec(memory_space=pltpu.VMEM)
    smem = pl.BlockSpec(memory_space=pltpu.SMEM)
    dma = pltpu.SemaphoreType.DMA
    return pl.pallas_call(
        functools.partial(kernel, (nodes, rels, chunks)),
        out_shape=jax.ShapeDtypeStruct((rels, rows // rels, width), jnp.float32),
        in_specs=[smem, smem, vmem, vmem, vmem, vmem] + [pl.BlockSpec(memory_space=pl.ANY)] * 2,
        out_specs=vmem,
        scratch_shapes=[
            pltpu.VMEM((row_tiles, slots, tile, tile), jnp.float32),
            pltpu.VMEM((nodes, rows, depth), jnp.float32),
            pltpu.VMEM((nodes, SUBLANES, tile), jnp.float32),
            pltpu.VMEM((rows, depth), jnp.float32),
            pltpu.VMEM((chunks, nodes, rows, LANES), jnp.float32),
            pltpu.VMEM((rows, LANES), jnp.float32),
            pltpu.VMEM((chunks, rows, LANES), jnp.float32),
            pltpu.VMEM((chunks, rows, LANES), jnp.float32),
            pltpu.VMEM((chunks, rows, LANES), jnp.float32),
            dma((2,)),
            dma((nodes,)),
            dma((nodes,)),
            dma((2, nodes, parts)),
            dma((nodes, parts)),
            dma((nodes, parts)),
            dma((nodes, parts)),
            dma((nodes, parts)),
            dma((nodes, parts)),
            dma((chunks,)),
            dma((chunks,)),
            dma((chunks, 2, nodes)),
            dma((chunks, nodes)),
            dma((chunks, rels)),
            dma((chunks, rels)),
        ],
        compiler_params=pltpu.CompilerParams(
            collective_id=0, has_side_effects=True, vmem_limit_bytes=56 << 20
        ),
    )(
        slot_of.reshape(-1),
        live.reshape(-1),
        source_scale,
        proj_weight[0],
        scale,
        proj_bias,
        features,
        tile_values[0],
    )


def solution(mesh):
    return jax.shard_map(
        functools.partial(on_device, mesh.shape["node"], mesh.shape["rel"]),
        mesh=mesh,
        in_specs=(
            P("node", "feat"),
            P("rel", "node", None, None, None),
            P("rel", "node", None),
            P("rel", "node"),
            P("rel", "node"),
            P("rel", "feat", None),
            P("rel", "feat"),
        ),
        out_specs=P(None, ("node", "rel"), "feat"),
        check_vma=False,
    )
```

time: 128 us -> 120 us (0.938)
  Pallas kernels: 121 us -> 113 us
    pallas_call x1, Pallas kernels: 121 us -> 113 us  [on_device(): pl.pallas_call(functools.partial(kernel, (nodes, rels, chunks)), out_shap...]
where the time goes in v3:
time: 120 us
  Pallas kernels  113 us (94%)
  local copies, waits for them, and re-layouts  5.45 us (5%)
  other arithmetic  1.67 us (1%)
    pallas_call x1, Pallas kernels, on_device(): pl.pallas_call(functools.partial(kernel, (nodes, rels, chunks)), out_shap...  113 us
    unnamed x2, local copies, waits for them, and re-layouts  2.74 us

profile of v3, /device:TPU:0, one launch (start us, length us, event | category | flops | bytes accessed | tf_op | source)
XLA Modules:
  0.0 119.9 jit_solution(9154990903352601005)
XLA Ops:
  0.0 0.7 iota_compare_fusion.1
  0.7 0.7 copy.10
  1.4 0.1 convert_reduce_fusion
  1.5 0.6 reshape.40.live
  2.1 0.1 select_reduce_fusion
  2.3 0.6 reshape.39.slot_of
  2.8 0.7 rsqrt_reduce_fusion
  3.6 0.6 pad.4.source_scale
  4.2 0.9 broadcast_in_dim.24.scale
  5.1 112.8 %shard_map.73 = f32[4,192,256]{2,1,0:T(8,128)} custom-call(s32[36]{0:T(128)} %reshape.39.slot_of, f32[36]{0:T(128)} %reshape.40.live, f32[8,256]{1,0:T(8,128)} %pad.4.source_scale, f32[384,512]{1,0:T(8,128)} %bitcast.7, f32[768,128]{1,0:T(8,128)} %broadcast_in_dim.24.scale, f32[1,256]{1,0:T(1,128)} %bias.1, f32[768,384]{1,0:T(8,128)} %features_hbm.1, ...), custom_call_target="tpu_custom_call" | custom-call | tf_op jit(solution)/shard_map/pallas_call | solution.py:385
  117.8 2.1 %copy.12 = f32[4,192,256]{2,1,0:T(8,128)} copy(f32[4,192,256]{2,1,0:T(8,128)} %shard_map.73) | data formatting | bytes 1572864
  (1 shorter events, 0.0 us)

commit v4 on v3

--- a/solution.py
+++ b/solution.py
@@ -32,15 +32,17 @@
 
 def kernel(
     sizes,
-    slot_of,
-    live,
-    source_scale,
+    tile_cols,
+    tile_count,
+    degree,
     weight,
-    scale,
     bias,
     features_hbm,
     tiles_hbm,
     out,
+    slot_of,
+    live,
+    scale,
     tiles,
     raw,
     scales,
@@ -67,12 +69,12 @@
     out_recv,
 ):
     nodes, rels, chunks = sizes
-    rows, depth = raw.shape[1:]
+    parts, rows = raw.shape[1:3]
+    slots = tiles.shape[1]
     tile = tiles.shape[2]
     row_tiles = tiles.shape[0]
     col_tiles = nodes * row_tiles
     group = rows // rels
-    parts = depth // LANES
     rel, node, feat = (lax.axis_index(name) for name in ("rel", "node", "feat"))
     has_up, has_down = node < nodes - 1, node > 0
     x_rel, y_rel, far_rel = rel + 1 - 2 * lax.rem(rel, 2), lax.rem(rel + 2, rels), rels - 1 - rel
@@ -85,12 +87,22 @@
     for step in range(1, nodes):
         peer = lax.rem(node + step, nodes)
         pl.semaphore_signal(barrier, inc=1, device_id={"node": peer}, device_id_type=MESH)
-    features_copy = pltpu.make_async_copy(features_hbm, raw.at[node], load_sem.at[0])
-    features_copy.start()
-    tiles_copy = pltpu.make_async_copy(tiles_hbm, tiles, load_sem.at[1])
+    features_copies = [
+        pltpu.make_async_copy(
+            features_hbm.at[:, pl.ds(p * LANES, LANES)], raw.at[node, p], load_sem.at[p]
+        )
+        for p in range(parts)
+    ]
+    for copy in features_copies:
+        copy.start()
+    tiles_copy = pltpu.make_async_copy(tiles_hbm, tiles, load_sem.at[parts])
     tiles_copy.start()
-    scales[node] = source_scale[...]
-    features_copy.wait()
+    row_scale = lax.rsqrt(degree[...].astype(jnp.float32))
+    scales[node] = jnp.zeros(scales.shape[1:], jnp.float32)
+    for t in range(row_tiles):
+        scales[node, t : t + 1, :] = row_scale[:, t * tile : (t + 1) * tile]
+    for copy in features_copies:
+        copy.wait()
     pl.semaphore_wait(barrier, rels + nodes - 1)
 
     def remote(src, dst, send_sem, recv_sem, **device):
@@ -111,7 +123,7 @@
 
     def piece(slot, quarter, part):
         place = pl.ds(pl.multiple_of(quarter * group, 8), group)
-        return raw.at[slot, place, pl.ds(part * LANES, LANES)]
+        return raw.at[slot, part, place, :]
 
     def z_copy(way, slot, p):
         ref = piece(slot, rel, p) if p < parts else piece(slot, far_rel, 0)
@@ -185,7 +197,8 @@
 
     def accumulate_first(slot):
         def one_tile(j, carry):
-            x = raw[slot, pl.ds(pl.multiple_of(j * tile, tile), tile), :]
+            place = pl.ds(pl.multiple_of(j * tile, tile), tile)
+            x = jnp.concatenate([raw[slot, p, place, :] for p in range(parts)], axis=1)
             x_high, x_pair = paired(x)
             column_scale = scales[slot, pl.ds(j, 1), :]
             for t in range(row_tiles):
@@ -195,6 +208,23 @@
             return carry
 
         lax.fori_loop(0, row_tiles, one_tile, 0)
+
+    for block in range(rows // LANES):
+        lanes = slice(block * LANES, (block + 1) * LANES)
+        scale[lanes, :] = jnp.broadcast_to(row_scale[:, lanes], (LANES, LANES)).T
+    for t in range(row_tiles):
+
+        def find(c, carry, t=t):
+            found, hits = jnp.int32(0), jnp.int32(0)
+            for k in range(slots):
+                hit = jnp.logical_and(tile_cols[0, t, k] == c, k < tile_count[0, t])
+                found += k * hit.astype(jnp.int32)
+                hits += hit.astype(jnp.int32)
+            slot_of[t * col_tiles + c] = found
+            live[t * col_tiles + c] = hits.astype(jnp.float32)
+            return carry
+
+        lax.fori_loop(0, col_tiles, find, 0)
 
     both_sides(1, take_z)
     first[...] = jnp.zeros_like(first)
@@ -370,26 +400,21 @@
     width = proj_bias.shape[1]
     chunks = width // LANES
     col_tiles = nodes * row_tiles
-    parts = depth // LANES + 1
-    row_scale = lax.rsqrt(degree[0].astype(jnp.float32))
-    scale = jnp.broadcast_to(row_scale[:, None], (rows, LANES))
-    source_scale = jnp.pad(row_scale.reshape(row_tiles, tile), ((0, SUBLANES - row_tiles), (0, 0)))
-    places = jnp.arange(slots)
-    used = places[None, :] < tile_count[0][:, None]
-    hit = (tile_cols[0][:, None, :] == jnp.arange(col_tiles)[None, :, None]) & used[:, None, :]
-    slot_of = jnp.sum(jnp.where(hit, places[None, None, :], 0), axis=2).astype(jnp.int32)
-    live = jnp.sum(hit.astype(jnp.float32), axis=2)
+    parts = depth // LANES
     vmem = pl.BlockSpec(memory_space=pltpu.VMEM)
     smem = pl.BlockSpec(memory_space=pltpu.SMEM)
     dma = pltpu.SemaphoreType.DMA
     return pl.pallas_call(
         functools.partial(kernel, (nodes, rels, chunks)),
         out_shape=jax.ShapeDtypeStruct((rels, rows // rels, width), jnp.float32),
-        in_specs=[smem, smem, vmem, vmem, vmem, vmem] + [pl.BlockSpec(memory_space=pl.ANY)] * 2,
+        in_specs=[smem, smem, vmem, vmem, vmem] + [pl.BlockSpec(memory_space=pl.ANY)] * 2,
         out_specs=vmem,
         scratch_shapes=[
+            pltpu.SMEM((row_tiles * col_tiles,), jnp.int32),
+            pltpu.SMEM((row_tiles * col_tiles,), jnp.float32),
+            pltpu.VMEM((rows, LANES), jnp.float32),
             pltpu.VMEM((row_tiles, slots, tile, tile), jnp.float32),
-            pltpu.VMEM((nodes, rows, depth), jnp.float32),
+            pltpu.VMEM((nodes, parts, rows, LANES), jnp.float32),
             pltpu.VMEM((nodes, SUBLANES, tile), jnp.float32),
             pltpu.VMEM((rows, depth), jnp.float32),
             pltpu.VMEM((chunks, nodes, rows, LANES), jnp.float32),
@@ -397,15 +422,15 @@
             pltpu.VMEM((chunks, rows, LANES), jnp.float32),
             pltpu.VMEM((chunks, rows, LANES), jnp.float32),
             pltpu.VMEM((chunks, rows, LANES), jnp.float32),
-            dma((2,)),
+            dma((parts + 1,)),
             dma((nodes,)),
             dma((nodes,)),
-            dma((2, nodes, parts)),
-            dma((nodes, parts)),
-            dma((nodes, parts)),
-            dma((nodes, parts)),
-            dma((nodes, parts)),
-            dma((nodes, parts)),
+            dma((2, nodes, parts + 1)),
+            dma((nodes, parts + 1)),
+            dma((nodes, parts + 1)),
+            dma((nodes, parts + 1)),
+            dma((nodes, parts + 1)),
+            dma((nodes, parts + 1)),
             dma((chunks,)),
             dma((chunks,)),
             dma((chunks, 2, nodes)),
@@ -417,11 +442,10 @@
             collective_id=0, has_side_effects=True, vmem_limit_bytes=56 << 20
         ),
     )(
-        slot_of.reshape(-1),
-        live.reshape(-1),
-        source_scale,
+        tile_cols,
+        tile_count,
+        degree,
         proj_weight[0],
-        scale,
         proj_bias,
         features,
         tile_values[0],

time: 120 us -> 116 us (0.967)
  local copies, waits for them, and re-layouts: 5.45 us -> 3.32 us
  other arithmetic: 1.67 us -> 0 us
where the time goes in v4:
time: 116 us
  Pallas kernels  113 us (97%)
  local copies, waits for them, and re-layouts  3.32 us (3%)
    pallas_call x1, Pallas kernels, on_device(): pl.pallas_call(functools.partial(kernel, (nodes, rels, chunks)), out_shap...  113 us
    unnamed x2, local copies, waits for them, and re-layouts  3.32 us

profile of v4, /device:TPU:0, one launch (start us, length us, event | category | flops | bytes accessed | tf_op | source)
XLA Modules:
  0.0 116.0 jit_solution(2929909751025069497)
XLA Ops:
  0.0 1.3 %copy.8.tile_cols = s32[1,3,12]{2,1,0:T(4,128)} copy(s32[1,3,12]{2,0,1:T(1,128)} %param.9) | data formatting | bytes 288 | tf_op args[2]
  1.3 112.7 %shard_map.73 = f32[4,192,256]{2,1,0:T(8,128)} custom-call(s32[1,3,12]{2,1,0:T(4,128)} %copy.8.tile_cols, s32[1,3]{1,0:T(1,128)} %tile_count.1, s32[1,768]{1,0:T(1,128)} %degree.1, f32[384,512]{1,0:T(8,128)} %bitcast.3, f32[1,256]{1,0:T(1,128)} %bias.1, f32[768,384]{1,0:T(8,128)} %features_hbm.1, f32[3,12,256,256]{3,2,1,0:T(8,128)} %bitcast.2), custom_call_target="tpu_custom_call" | custom-call | tf_op jit(solution)/shard_map/pallas_call | solution.py:407
  113.9 2.1 %copy.10 = f32[4,192,256]{2,1,0:T(8,128)} copy(f32[4,192,256]{2,1,0:T(8,128)} %shard_map.73) | data formatting | bytes 1572864

commit v5 on v4

--- a/solution.py
+++ b/solution.py
@@ -150,29 +150,35 @@
     def y_in(slot, p):
         return y_copy(slot, p, y_rel, far_rel)
 
-    def take_z(way, slot):
-        onward = has_up if way == 0 else has_down
+    def take_z(way, slot, p):
+        z_copy(way, slot, p).wait_recv()
+
+        @pl.when(has_up if way == 0 else has_down)
+        def _():
+            z_copy(way, slot, p).start()
+
+        if p < parts:
+            x_out(slot, p).start()
+            y_out(slot, p).start()
+
+    def take_nearest(way, slot):
         for p in range(parts + 1):
-            z_copy(way, slot, p).wait_recv()
-
-            @pl.when(onward)
+            take_z(way, slot, p)
+
+    def advance(way, slot):
+        beyond = slot - 1 if way == 0 else slot + 1
+        for p in range(parts + 1):
+
+            @pl.when(slot > 0 if way == 0 else slot < nodes - 1)
             def _(p=p):
-                z_copy(way, slot, p).start()
-
-            if p < parts:
-                x_out(slot, p).start()
-                y_out(slot, p).start()
-
-    def take_xy(slot):
-        for p in range(parts):
+                take_z(way, beyond, p)
+
             x_in(slot, p).wait_recv()
             if p == 2:
                 y_out(slot, parts).start()
             y_in(slot, p).wait_recv()
             if p == 1:
                 x_out(slot, parts).start()
-        x_in(slot, parts).wait_recv()
-        y_in(slot, parts).wait_recv()
 
     def both_sides(s, act):
         @pl.when(node - s >= 0)
@@ -226,14 +232,13 @@
 
         lax.fori_loop(0, col_tiles, find, 0)
 
-    both_sides(1, take_z)
+    both_sides(1, take_nearest)
     first[...] = jnp.zeros_like(first)
     tiles_copy.wait()
     accumulate_first(node)
 
     def first_step(s, carry):
-        both_sides(s + 1, take_z)
-        both_sides(s, lambda way, slot: take_xy(slot))
+        both_sides(s, advance)
 
         def use(way, slot):
             scale_copy(slot, 1).wait_recv()

time: 116 us -> 116 us (level)
  no operation moved by 1% of the time
where the time goes in v5:
time: 116 us
  Pallas kernels  113 us (97%)
  local copies, waits for them, and re-layouts  3.32 us (3%)
    pallas_call x1, Pallas kernels, on_device(): pl.pallas_call(functools.partial(kernel, (nodes, rels, chunks)), out_shap...  113 us
    unnamed x2, local copies, waits for them, and re-layouts  3.32 us

profile of v5, /device:TPU:0, one launch (start us, length us, event | category | flops | bytes accessed | tf_op | source)
XLA Modules:
  0.0 116.1 jit_solution(7165784657138458909)
XLA Ops:
  0.0 1.3 %copy.8.tile_cols = s32[1,3,12]{2,1,0:T(4,128)} copy(s32[1,3,12]{2,0,1:T(1,128)} %param.9) | data formatting | bytes 288 | tf_op args[2]
  1.3 112.8 %shard_map.73 = f32[4,192,256]{2,1,0:T(8,128)} custom-call(s32[1,3,12]{2,1,0:T(4,128)} %copy.8.tile_cols, s32[1,3]{1,0:T(1,128)} %tile_count.1, s32[1,768]{1,0:T(1,128)} %degree.1, f32[384,512]{1,0:T(8,128)} %bitcast.3, f32[1,256]{1,0:T(1,128)} %bias.1, f32[768,384]{1,0:T(8,128)} %features_hbm.1, f32[3,12,256,256]{3,2,1,0:T(8,128)} %bitcast.2), custom_call_target="tpu_custom_call" | custom-call | tf_op jit(solution)/shard_map/pallas_call | solution.py:412
  114.0 2.1 %copy.10 = f32[4,192,256]{2,1,0:T(8,128)} copy(f32[4,192,256]{2,1,0:T(8,128)} %shard_map.73) | data formatting | bytes 1572864

commit v6 on v4

--- a/solution.py
+++ b/solution.py
@@ -209,6 +209,7 @@
 
         lax.fori_loop(0, row_tiles, one_tile, 0)
 
+    both_sides(1, take_z)
     for block in range(rows // LANES):
         lanes = slice(block * LANES, (block + 1) * LANES)
         scale[lanes, :] = jnp.broadcast_to(row_scale[:, lanes], (LANES, LANES)).T
@@ -226,7 +227,6 @@
 
         lax.fori_loop(0, col_tiles, find, 0)
 
-    both_sides(1, take_z)
     first[...] = jnp.zeros_like(first)
     tiles_copy.wait()
     accumulate_first(node)

time: 116 us -> 116 us (level)
  no operation moved by 1% of the time
where the time goes in v6:
time: 116 us
  Pallas kernels  113 us (97%)
  local copies, waits for them, and re-layouts  3.32 us (3%)
    pallas_call x1, Pallas kernels, on_device(): pl.pallas_call(functools.partial(kernel, (nodes, rels, chunks)), out_shap...  113 us
    unnamed x2, local copies, waits for them, and re-layouts  3.32 us

profile of v6, /device:TPU:0, one launch (start us, length us, event | category | flops | bytes accessed | tf_op | source)
XLA Modules:
  0.0 116.0 jit_solution(16854910240694403105)
XLA Ops:
  0.0 1.3 %copy.8.tile_cols = s32[1,3,12]{2,1,0:T(4,128)} copy(s32[1,3,12]{2,0,1:T(1,128)} %param.9) | data formatting | bytes 288 | tf_op args[2]
  1.3 112.7 %shard_map.73 = f32[4,192,256]{2,1,0:T(8,128)} custom-call(s32[1,3,12]{2,1,0:T(4,128)} %copy.8.tile_cols, s32[1,3]{1,0:T(1,128)} %tile_count.1, s32[1,768]{1,0:T(1,128)} %degree.1, f32[384,512]{1,0:T(8,128)} %bitcast.3, f32[1,256]{1,0:T(1,128)} %bias.1, f32[768,384]{1,0:T(8,128)} %features_hbm.1, f32[3,12,256,256]{3,2,1,0:T(8,128)} %bitcast.2), custom_call_target="tpu_custom_call" | custom-call | tf_op jit(solution)/shard_map/pallas_call | solution.py:407
  113.9 2.1 %copy.10 = f32[4,192,256]{2,1,0:T(8,128)} copy(f32[4,192,256]{2,1,0:T(8,128)} %shard_map.73) | data formatting | bytes 1572864
